TPU v7x, 32 devices: a whole 2x2x4 slice. The times are simulated.
32 devices in a mesh: gz: 2 (over x), gy: 4 (over y, core), gx: 4 (over z).
Axes of the slice: x: 2, y: 2, z: 4, core: 2. Of those that a mesh axis runs over, the one named last changes fastest.
Arguments:
- pressure: float32 [8, 512, 512], P('gz', 'gy', 'gx'), may hold values from -6 to 6
- light: float32 [4, 3], replicated, may hold values from -4 to 4
- palette: float32 [3, 2], replicated, may hold values from -4 to 4
- rate: float32 [4], replicated, may hold values from 0.0625 to 0.375
- shear: int32 [4, 8, 2], replicated, may hold values from 0 to 8
- offset: int32 [4, 2, 2], replicated, may hold values from 0 to 31
- order: int32 [4, 2], replicated, may hold values from 0 to 1, each once within a row
Outputs:
- picture: float32 [4, 4, 2, 256, 512], P(None, None, 'gz', 'gy', 'gx')
Inputs may be any that keep to these rules, and one draw needn't show every extreme that they name: `order`: each row is a permutation of 0 to 1.
All inputs are finite; a program needn't handle non-finite values.
Results may differ from a plain program's by a relative error of at most 0.00005.
Values sent between devices are 32-bit elements; how exact they have to be, the bound alone decides.
A program may use at most 64 MiB of HBM per device.

v0:
```python
import jax
import jax.numpy as jnp
from jax import lax
from jax.sharding import PartitionSpec as P

VIEWS = 4
SHEAR = 8
REACH = 32


def padded(cells, sides, width):
    for axis, dim in sides:
        count = lax.axis_size(axis)
        ends = count - 1
        head = lax.slice_in_dim(cells, 0, width, axis=dim)
        tail = lax.slice_in_dim(cells, cells.shape[dim] - width, cells.shape[dim], axis=dim)
        cells = jnp.concatenate(
            [
                lax.ppermute(tail, axis, [(i, (i + 1) % count) for i in range(ends)]),
                cells,
                lax.ppermute(head, axis, [((i + 1) % count, i) for i in range(ends)]),
            ],
            axis=dim,
        )
    return cells


def shifted(value, axis, steps):
    count = lax.axis_size(axis)
    first, last = (max(0, -steps), min(count, count - steps))
    return lax.ppermute(value, axis, [(source, source + steps) for source in range(first, last)])


def surface_terms(slab):
    inner = slab[1:-1, 1:-1, 1:-1]
    grad_depth = 0.5 * (slab[2:, 1:-1, 1:-1] - slab[:-2, 1:-1, 1:-1])
    grad_rows = 0.5 * (slab[1:-1, 2:, 1:-1] - slab[1:-1, :-2, 1:-1])
    grad_cols = 0.5 * (slab[1:-1, 1:-1, 2:] - slab[1:-1, 1:-1, :-2])
    factor = lax.rsqrt(
        grad_depth * grad_depth + grad_rows * grad_rows + grad_cols * grad_cols + 1.0
    )
    return (inner, (grad_depth * factor, grad_rows * factor, grad_cols * factor))


def render_layers(inner, normals, shifts, light, palette, rate, rows, cols):
    lengths = jnp.sqrt(jnp.sum(light * light, axis=1, keepdims=True) + 1.0)
    towards = light / lengths
    offsets = palette[:, 0][:, None, None]
    slopes = palette[:, 1][:, None, None]
    layers = []
    for view in range(light.shape[0]):

        def advance(carry, items):
            color, depth = carry
            value_slab, normal_depth, normal_rows, normal_cols, moved = items
            start = (SHEAR - moved[0], SHEAR - moved[1])
            value = lax.dynamic_slice(value_slab, start, (rows, cols))
            dot = (
                lax.dynamic_slice(normal_depth, start, (rows, cols)) * towards[view, 0]
                + lax.dynamic_slice(normal_rows, start, (rows, cols)) * towards[view, 1]
                + lax.dynamic_slice(normal_cols, start, (rows, cols)) * towards[view, 2]
            )
            shade = 0.25 + 0.75 * dot * dot
            density = rate[view] * (1.0 + jnp.tanh(value))
            alpha = 1.0 - jnp.exp(-density)
            weight = alpha * jnp.exp(-depth)
            hues = jax.nn.sigmoid(offsets + slopes * value[None]) * shade[None]
            return ((color + hues * weight[None], depth + density), None)

        start_carry = (
            jnp.zeros((3, rows, cols), jnp.float32),
            jnp.zeros((rows, cols), jnp.float32),
        )
        (color, depth), _ = lax.scan(
            advance, start_carry, (inner, normals[0], normals[1], normals[2], shifts[view])
        )
        layers.append(jnp.concatenate([color, depth[None]], axis=0))
    return jnp.stack(layers)


def precedence(order):
    bricks = order.shape[1]
    onehot = (order[:, :, None] == jnp.arange(bricks, dtype=jnp.int32)[None, None, :]).astype(
        jnp.float32
    )
    ranks = jnp.sum(onehot * jnp.arange(bricks, dtype=jnp.float32)[None, :, None], axis=1)
    return (ranks[:, None, :] < ranks[:, :, None]).astype(jnp.float32)


def on_device(pressure, light, palette, rate, shear, offset, order):
    depth_cells, rows, cols = pressure.shape
    brick = lax.axis_index("gz")
    zero = jnp.zeros((), jnp.int32)
    widened = padded(pressure, (("gy", 1), ("gx", 2)), SHEAR + 1)
    slab = padded(widened, (("gz", 0),), 1)
    inner, normals = surface_terms(slab)
    shifts = lax.dynamic_slice(shear, (zero, brick * depth_cells, zero), (VIEWS, depth_cells, 2))
    layers = render_layers(inner, normals, shifts, light, palette, rate, rows, cols)
    moved = lax.dynamic_index_in_dim(offset, brick, 1, keepdims=False)
    blank = jnp.zeros((4, rows + REACH, cols + REACH), jnp.float32)
    canvas = jnp.stack(
        [
            lax.dynamic_update_slice(blank, layers[view], (zero, moved[view, 0], moved[view, 1]))
            for view in range(VIEWS)
        ]
    )
    own_tile = canvas[:, :, :rows, :cols]
    from_above = shifted(canvas[:, :, rows:, :cols], "gy", 1)
    from_left = shifted(canvas[:, :, :rows, cols:], "gx", 1)
    from_diagonal = shifted(canvas[:, :, rows:, cols:], ("gy", "gx"), lax.axis_size("gx") + 1)
    from_diagonal = from_diagonal * (lax.axis_index("gx") > 0).astype(jnp.float32)
    own_tile = own_tile.at[:, :, :REACH, :].add(from_above)
    own_tile = own_tile.at[:, :, :, :REACH].add(from_left)
    own_tile = own_tile.at[:, :, :REACH, :REACH].add(from_diagonal)
    ranking = precedence(order)
    pieces = lax.all_to_all(own_tile[None], "gz", split_axis=3, concat_axis=0, tiled=True)
    depths = pieces[:, :, 3]
    cover = jnp.einsum("vbc,cvyx->bvyx", ranking, depths, precision=lax.Precision.HIGHEST)
    colors = jnp.sum(pieces[:, :, :3] * jnp.exp(-cover)[:, :, None], axis=0)
    opacity = 1.0 - jnp.exp(-jnp.sum(depths, axis=0))
    image = jnp.concatenate([colors, opacity[:, None]], axis=1)
    return image[:, :, None]


def solution(mesh):
    return jax.shard_map(
        on_device,
        mesh=mesh,
        in_specs=(P("gz", "gy", "gx"), P(), P(), P(), P(), P(), P()),
        out_specs=P(None, None, "gz", "gy", "gx"),
        check_vma=False,
    )
```

profile of v0, /device:TPU:0, one launch (start us, length us, event | category | flops | bytes accessed | tf_op | source)
XLA Modules:
  0.0 226.7 jit_solution(1178924333842088694)
XLA Ops:
  2.1 3.0 %collective-permute-start = (f32[4,9,128]{2,1,0:T(8,128)S(1)}, f32[4,9,128]{2,1,0:T(8,128)S(1)}, u32[]{:S(2)}, u32[]{:S(2)}) collective-permute-start(f32[4,9,128]{2,1,0:T(8,128)S(1)} %get-tuple-element.1122), channel_id=1, source_target_pairs={{0,4},{4,8},{8,12},{1,5},{5,9},{9,13},{2,6},{6,10},{10,14},{3,7},{... | collective-permute-start | bytes 55304 | tf_op jit(solution)/shard_map/ppermute | solution.py:19
  10.0 5.6 %collective-permute-start.2 = (f32[4,146,9]{2,1,0:T(8,128)S(1)}, f32[4,146,9]{2,1,0:T(8,128)S(1)}, u32[]{:S(2)}, u32[]{:S(2)}) collective-permute-start(f32[4,146,9]{2,1,0:T(8,128)S(1)} %get-tuple-element.1120), channel_id=1, source_target_pairs={{0,1},{1,2},{2,3},{4,5},{5,6},{6,7},{8,9},{9,10},{10,11},{12,13},{... | collective-permute-start | bytes 63080 | tf_op jit(solution)/shard_map/ppermute | solution.py:19
  32.8 4.0 %collective-permute-start.5 = (f32[1,146,146]{2,1,0:T(8,128)S(1)}, f32[1,146,146]{2,1,0:T(8,128)S(1)}, u32[]{:S(2)}, u32[]{:S(2)}) collective-permute-start(f32[1,146,146]{2,1,0:T(8,128)S(1)} %get-tuple-element.1118), channel_id=1, source_target_pairs={{0,16},{1,17},{2,18},{3,19},{4,20},{5,21},{6,22},{7,23},{8,24},{9,... | collective-permute-start | bytes 255800 | tf_op jit(solution)/shard_map/ppermute | solution.py:19
  38.2 2.6 %collective-permute-done.5 = f32[1,146,146]{2,1,0:T(8,128)S(1)} collective-permute-done((f32[1,146,146]{2,1,0:T(8,128)S(1)}, f32[1,146,146]{2,1,0:T(8,128)S(1)}, u32[]{:S(2)}, u32[]{:S(2)}) %collective-permute-start.5) | collective-permute-done | bytes 85296 | tf_op jit(solution)/shard_map/ppermute | solution.py:19
  40.8 4.1 %collective-permute-done.4 = f32[1,146,146]{2,1,0:T(8,128)S(1)} collective-permute-done((f32[1,146,146]{2,1,0:T(8,128)S(1)}, f32[1,146,146]{2,1,0:T(8,128)S(1)}, u32[]{:S(2)}, u32[]{:S(2)}) %collective-permute-start.4) | collective-permute-done | bytes 85296 | tf_op jit(solution)/shard_map/ppermute | solution.py:21
  46.0 2.4 %fusion.19 = (f32[4,144,144]{2,1,0:T(8,128)S(1)}, f32[4,144,144]{2,1,0:T(8,128)S(1)}, f32[4,144,144]{2,1,0:T(8,128)S(1)}) fusion(f32[4,144,144]{2,1,0:T(8,128)S(1)} %get-tuple-element.1094, f32[4,146,146]{2,1,0:T(8,128)S(1)} %pad_maximum_fusion.1, f32[4,146,9]{2,1,0:T(8,128)} %copy-done.6, f32[4,9,128]{2,1,0:T(8,128)S(1)} %collective-permute-done.1, ...), kind=kLoop, calls=%fused_computation.77 | loop fusion | flops 1327104 | bytes 2834016 | tf_op jit(solution)/shard_map/mul | solution.py:42
  48.4 31.0 %while.70 = (s32[]{:T(128)}, f32[3,128,128]{2,1,0:T(8,128)S(1)}, f32[128,128]{1,0:T(8,128)S(1)}, f32[3,1,1]{0,2,1:T(1,128)S(1)}, f32[3,1,1]{0,2,1:T(1,128)S(1)},...) while((s32[]{:T(128)}, f32[3,128,128]{2,1,0:T(8,128)S(1)}, ...), condition=%wide.region_8.9_spmd.clone, body=%wide.region_7.8_spmd.clone.sunk | while | flops 753678 | bytes 1442253 | solution.py:74
  54.1 1.9 fusion.67
  61.8 1.9 fusion.67
  69.6 1.9 fusion.67
  77.3 1.9 fusion.67
  79.4 31.0 %while.69 = (s32[]{:T(128)}, f32[3,128,128]{2,1,0:T(8,128)S(1)}, f32[128,128]{1,0:T(8,128)S(1)}, f32[3,1,1]{0,2,1:T(1,128)S(1)}, f32[3,1,1]{0,2,1:T(1,128)S(1)},...) while((s32[]{:T(128)}, f32[3,128,128]{2,1,0:T(8,128)S(1)}, ...), condition=%wide.region_6.7_spmd.clone, body=%wide.region_5.6_spmd.clone.sunk | while | flops 753678 | bytes 1442253 | solution.py:74
  85.1 1.9 fusion.64
  92.8 1.9 fusion.64
  100.5 1.9 fusion.64
  108.3 1.9 fusion.64
  110.4 31.0 %while.68 = (s32[]{:T(128)}, f32[3,128,128]{2,1,0:T(8,128)S(1)}, f32[128,128]{1,0:T(8,128)S(1)}, f32[3,1,1]{0,2,1:T(1,128)S(1)}, f32[3,1,1]{0,2,1:T(1,128)S(1)},...) while((s32[]{:T(128)}, f32[3,128,128]{2,1,0:T(8,128)S(1)}, ...), condition=%wide.region_4.5_spmd.clone, body=%wide.region_3.4_spmd.clone.sunk | while | flops 753678 | bytes 1442253 | solution.py:74
  116.0 1.9 fusion.61
  123.8 1.9 fusion.61
  131.5 1.9 fusion.61
  139.3 1.9 fusion.61
  141.4 24.5 %while.67 = (s32[]{:T(128)}, f32[3,128,128]{2,1,0:T(8,128)S(1)}, f32[128,128]{1,0:T(8,128)S(1)}, f32[3,1,1]{0,2,1:T(1,128)S(1)}, f32[3,1,1]{0,2,1:T(1,128)S(1)},...) while((s32[]{:T(128)}, f32[3,128,128]{2,1,0:T(8,128)S(1)}, ...), condition=%wide.region_2.3_spmd.clone, body=%wide.region_1.2_spmd.clone.sunk | while | flops 753678 | bytes 1442245 | solution.py:74
  157.6 1.9 fusion.58
  166.1 3.1 %dynamic_update_slice.19 = f32[1,4,160,160]{3,2,1,0:T(8,128)S(1)} dynamic-update-slice(f32[1,4,160,160]{3,2,1,0:T(8,128)S(1)} %broadcast_in_dim.30.clone, f32[1,4,128,128]{3,2,1,0:T(8,128)S(1)} %maximum_bitcast_fusion.4, s32[]{:T(128)} %constant.961.clone.1, s32[]{:T(128)} %constant.961.clone.1, s32[]{:T(128)S(6)} %select_n.135, s32[]{:T(128)S(6)} %select_n.136) | dynamic-update-slice | bytes 524292 | tf_op jit(solution)/shard_map/dynamic_update_slice | solution.py:103
  170.8 3.1 %dynamic_update_slice.17 = f32[1,4,160,160]{3,2,1,0:T(8,128)S(1)} dynamic-update-slice(f32[1,4,160,160]{3,2,1,0:T(8,128)S(1)} %broadcast_in_dim.30.clone.2, f32[1,4,128,128]{3,2,1,0:T(8,128)S(1)} %maximum_bitcast_fusion.2, s32[]{:T(128)} %constant.961.clone.1, s32[]{:T(128)} %constant.961.clone.1, s32[]{:T(128)S(6)} %select_n.131, s32[]{:T(128)S(6)} %select_n.132) | dynamic-update-slice | bytes 524292 | tf_op jit(solution)/shard_map/dynamic_update_slice | solution.py:103
  174.0 3.1 %dynamic_update_slice.16 = f32[1,4,160,160]{3,2,1,0:T(8,128)S(1)} dynamic-update-slice(f32[1,4,160,160]{3,2,1,0:T(8,128)S(1)} %broadcast_in_dim.30.clone.3, f32[1,4,128,128]{3,2,1,0:T(8,128)S(1)} %maximum_bitcast_fusion.1, s32[]{:T(128)} %constant.961.clone.1, s32[]{:T(128)} %constant.961.clone.1, s32[]{:T(128)S(6)} %select_n.129, s32[]{:T(128)S(6)} %select_n.130) | dynamic-update-slice | bytes 524292 | tf_op jit(solution)/shard_map/dynamic_update_slice | solution.py:103
  181.4 3.5 %collective-permute-start.7 = (f32[4,4,128,32]{2,3,1,0:T(8,128)S(1)}, f32[4,4,128,32]{2,3,1,0:T(8,128)S(1)}, u32[]{:S(2)}, u32[]{:S(2)}) collective-permute-start(f32[4,4,128,32]{2,3,1,0:T(8,128)S(1)} %copy.31), channel_id=1, source_target_pairs={{0,1},{1,2},{2,3},{4,5},{5,6},{6,7},{8,9},{9,10},{10,11},{12,13},{... | collective-permute-start | bytes 786440 | tf_op jit(solution)/shard_map/ppermute | solution.py:31
  186.9 2.3 %slice.439 = f32[4,4,128,128]{3,2,1,0:T(8,128)} slice(f32[4,4,160,160]{3,2,1,0:T(8,128)} %copy-done.2), slice={[0:4], [0:4], [0:128], [0:128]} | slice | bytes 2097152 | tf_op jit(solution)/shard_map/slice | solution.py:107
  190.0 5.5 %collective-permute-start.8 = (f32[4,4,32,32]{3,2,1,0:T(8,128)}, f32[4,4,32,32]{3,2,1,0:T(8,128)}, u32[]{:S(2)}, u32[]{:S(2)}) collective-permute-start(f32[4,4,32,32]{3,2,1,0:T(8,128)} %pad_maximum_fusion.13), channel_id=1, source_target_pairs={{0,5},{1,6},{2,7},{3,8},{4,9},{5,10},{6,11},{7,12},{8,13},{9,14},{... | collective-permute-start | bytes 196616 | tf_op jit(solution)/shard_map/ppermute | solution.py:31
  199.7 2.0 scatter-add.11
  205.4 3.6 %all-to-all-start = ((f32[1,4,4,128,128]{4,2,1,0,3:T(4,128)}), f32[1,4,4,128,128]{4,2,1,0,3:T(4,128)S(1)}, u32[]{:S(2)}, u32[]{:S(2)}) async-start(f32[1,4,4,128,128]{4,2,1,0,3:T(4,128)} %copy.33), calls=%async_computation | async-start | bytes 2097152 | tf_op jit(solution)/shard_map/all_to_all | solution.py:116
  209.1 13.7 %all-to-all-done = f32[1,4,4,128,128]{4,2,1,0,3:T(4,128)S(1)} async-done(((f32[1,4,4,128,128]{4,2,1,0,3:T(4,128)}), f32[1,4,4,128,128]{4,2,1,0,3:T(4,128)S(1)}, u32[]{:S(2)}, u32[]{:S(2)}) %all-to-all-start) | async-done | bytes 1048608 | tf_op jit(solution)/shard_map/all_to_all | solution.py:116
  (210 shorter events, 85.4 us)
Async XLA Ops:
  0.0 7.5 %copy-start = (s32[4,2,2]{0,2,1:T(2,128)S(1)}, s32[4,2,2]{0,2,1:T(2,128)}, u32[]{:S(2)}) copy-start(s32[4,2,2]{0,2,1:T(2,128)} %param.26) | copy-start | bytes 196
  0.0 44.9 %copy-start.3 = (f32[4,128,128]{2,1,0:T(8,128)S(1)}, f32[4,128,128]{2,1,0:T(8,128)}, u32[]{:S(2)}) copy-start(f32[4,128,128]{2,1,0:T(8,128)} %param.21) | copy-start | bytes 786436
  0.0 38.1 %copy-start.9 = (s32[4,8,2]{1,2,0:T(2,128)S(1)}, s32[4,8,2]{1,2,0:T(2,128)}, u32[]{:S(2)}) copy-start(s32[4,8,2]{1,2,0:T(2,128)} %param.25) | copy-start | bytes 772
  0.8 6.7 %collective-permute-start.1 = (f32[4,9,128]{2,1,0:T(8,128)S(1)}, f32[4,9,128]{2,1,0:T(8,128)S(1)}, u32[]{:S(2)}, u32[]{:S(2)}) collective-permute-start(f32[4,9,128]{2,1,0:T(8,128)S(1)} %get-tuple-element.1123), channel_id=1, source_target_pairs={{4,0},{8,4},{12,8},{5,1},{9,5},{13,9},{6,2},{10,6},{14,10},{7,3},{... | collective-permute-start | bytes 55304 | tf_op jit(solution)/shard_map/ppermute | solution.py:21
  2.1 5.4 %collective-permute-start = (f32[4,9,128]{2,1,0:T(8,128)S(1)}, f32[4,9,128]{2,1,0:T(8,128)S(1)}, u32[]{:S(2)}, u32[]{:S(2)}) collective-permute-start(f32[4,9,128]{2,1,0:T(8,128)S(1)} %get-tuple-element.1122), channel_id=1, source_target_pairs={{0,4},{4,8},{8,12},{1,5},{5,9},{9,13},{2,6},{6,10},{10,14},{3,7},{... | collective-permute-start | bytes 55304 | tf_op jit(solution)/shard_map/ppermute | solution.py:19
  8.7 22.6 %collective-permute-start.3 = (f32[4,146,9]{2,1,0:T(8,128)S(1)}, f32[4,146,9]{2,1,0:T(8,128)S(1)}, u32[]{:S(2)}, u32[]{:S(2)}) collective-permute-start(f32[4,146,9]{2,1,0:T(8,128)S(1)} %get-tuple-element.1121), channel_id=1, source_target_pairs={{1,0},{2,1},{3,2},{5,4},{6,5},{7,6},{9,8},{10,9},{11,10},{13,12},{... | collective-permute-start | bytes 63080 | tf_op jit(solution)/shard_map/ppermute | solution.py:21
  10.0 21.3 %collective-permute-start.2 = (f32[4,146,9]{2,1,0:T(8,128)S(1)}, f32[4,146,9]{2,1,0:T(8,128)S(1)}, u32[]{:S(2)}, u32[]{:S(2)}) collective-permute-start(f32[4,146,9]{2,1,0:T(8,128)S(1)} %get-tuple-element.1120), channel_id=1, source_target_pairs={{0,1},{1,2},{2,3},{4,5},{5,6},{6,7},{8,9},{9,10},{10,11},{12,13},{... | collective-permute-start | bytes 63080 | tf_op jit(solution)/shard_map/ppermute | solution.py:19
  31.2 14.8 %copy-start.6 = (f32[4,146,9]{2,1,0:T(8,128)}, f32[4,146,9]{2,1,0:T(8,128)S(1)}, u32[]{:S(2)}) copy-start(f32[4,146,9]{2,1,0:T(8,128)S(1)} %collective-permute-done.3) | copy-start | bytes 63076
  31.3 14.8 %copy-start.7 = (f32[4,146,9]{2,1,0:T(8,128)}, f32[4,146,9]{2,1,0:T(8,128)S(1)}, u32[]{:S(2)}) copy-start(f32[4,146,9]{2,1,0:T(8,128)S(1)} %collective-permute-done.2) | copy-start | bytes 63076
  32.7 13.3 %copy-start.4 = (f32[4,128,128]{2,1,0:T(8,128)S(1)}, f32[4,128,128]{2,1,0:T(8,128)}, u32[]{:S(2)}) copy-start(f32[4,128,128]{2,1,0:T(8,128)} %param.21) | copy-start | bytes 786436
  32.8 8.0 %collective-permute-start.5 = (f32[1,146,146]{2,1,0:T(8,128)S(1)}, f32[1,146,146]{2,1,0:T(8,128)S(1)}, u32[]{:S(2)}, u32[]{:S(2)}) collective-permute-start(f32[1,146,146]{2,1,0:T(8,128)S(1)} %get-tuple-element.1118), channel_id=1, source_target_pairs={{0,16},{1,17},{2,18},{3,19},{4,20},{5,21},{6,22},{7,23},{8,24},{9,... | collective-permute-start | bytes 255800 | tf_op jit(solution)/shard_map/ppermute | solution.py:19
  36.8 8.1 %collective-permute-start.4 = (f32[1,146,146]{2,1,0:T(8,128)S(1)}, f32[1,146,146]{2,1,0:T(8,128)S(1)}, u32[]{:S(2)}, u32[]{:S(2)}) collective-permute-start(f32[1,146,146]{2,1,0:T(8,128)S(1)} %get-tuple-element.1117), channel_id=1, source_target_pairs={{16,0},{17,1},{18,2},{19,3},{20,4},{21,5},{22,6},{23,7},{24,8},{25... | collective-permute-start | bytes 255800 | tf_op jit(solution)/shard_map/ppermute | solution.py:21
  46.0 2.4 %copy-start.8 = (f32[4]{0:T(128)S(1)}, f32[4]{0:T(128)}, u32[]{:S(2)}) copy-start(f32[4]{0:T(128)} %param.24) | copy-start | bytes 52
  177.3 1.5 copy-start.2
  181.4 14.1 %collective-permute-start.7 = (f32[4,4,128,32]{2,3,1,0:T(8,128)S(1)}, f32[4,4,128,32]{2,3,1,0:T(8,128)S(1)}, u32[]{:S(2)}, u32[]{:S(2)}) collective-permute-start(f32[4,4,128,32]{2,3,1,0:T(8,128)S(1)} %copy.31), channel_id=1, source_target_pairs={{0,1},{1,2},{2,3},{4,5},{5,6},{6,7},{8,9},{9,10},{10,11},{12,13},{... | collective-permute-start | bytes 786440 | tf_op jit(solution)/shard_map/ppermute | solution.py:31
  185.6 11.2 %collective-permute-start.6 = (f32[4,4,32,128]{3,2,1,0:T(8,128)}, f32[4,4,32,128]{3,2,1,0:T(8,128)S(1)}, u32[]{:S(2)}, u32[]{:S(2)}) collective-permute-start(f32[4,4,32,128]{3,2,1,0:T(8,128)} %pad_maximum_fusion.14), channel_id=1, source_target_pairs={{0,4},{4,8},{8,12},{1,5},{5,9},{9,13},{2,6},{6,10},{10,14},{3,7},{... | collective-permute-start | bytes 786440 | tf_op jit(solution)/shard_map/ppermute | solution.py:31
  190.0 11.7 %collective-permute-start.8 = (f32[4,4,32,32]{3,2,1,0:T(8,128)}, f32[4,4,32,32]{3,2,1,0:T(8,128)}, u32[]{:S(2)}, u32[]{:S(2)}) collective-permute-start(f32[4,4,32,32]{3,2,1,0:T(8,128)} %pad_maximum_fusion.13), channel_id=1, source_target_pairs={{0,5},{1,6},{2,7},{3,8},{4,9},{5,10},{6,11},{7,12},{8,13},{9,14},{... | collective-permute-start | bytes 196616 | tf_op jit(solution)/shard_map/ppermute | solution.py:31
  196.8 1.3 copy-start.5
  198.1 1.5 copy-start.1
  201.7 7.3 %copy-start.10 = (s32[4,2]{0,1:T(2,128)S(1)}, s32[4,2]{0,1:T(2,128)}, u32[]{:S(2)}) copy-start(s32[4,2]{0,1:T(2,128)} %param.27) | copy-start | bytes 100
  205.4 17.5 %all-to-all-start = ((f32[1,4,4,128,128]{4,2,1,0,3:T(4,128)}), f32[1,4,4,128,128]{4,2,1,0,3:T(4,128)S(1)}, u32[]{:S(2)}, u32[]{:S(2)}) async-start(f32[1,4,4,128,128]{4,2,1,0,3:T(4,128)} %copy.33), calls=%async_computation | async-start | bytes 2097152 | tf_op jit(solution)/shard_map/all_to_all | solution.py:116
where the time goes:
time: 230 us; the launch traced here: 227 us
  other arithmetic  65.6 us (29%)
  local copies, waits for them, and re-layouts  55.3 us (24%)
  loops' own time  39 us (17%)
  starting transfers between devices  30.3 us (13%)
  waiting for transfers between devices  20.5 us (9%)
  between operations  15.4 us (7%)
    another operation x4, loops' own time, render_layers(): lax.scan(advance, start_carry, (inner, normals[0], normals[1], normals[2]...  39 us
    mul x16, other arithmetic, advance(): hues = jax.nn.sigmoid(offsets + slopes * value[None]) * shade[None]  31 us
    all_to_all x1, waiting for transfers between devices, on_device(): lax.all_to_all(own_tile[None], 'gz', split_axis=3, concat_axis=0, tiled=T...  13.7 us
    ppermute x3, starting transfers between devices, padded(): lax.ppermute(tail, axis, [(i, (i + 1) % count) for i in range(ends)])  12.6 us
    add x32, other arithmetic, advance(): return ((color + hues * weight[None], depth + density), None)  12 us
    dynamic_update_slice x4, local copies, waits for them, and re-layouts, on_device(): lax.dynamic_update_slice(blank, layers[view], (zero, moved[view, 0], move...  10.8 us
    ppermute x3, starting transfers between devices, shifted(): lax.ppermute(value, axis, [(source, source + steps) for source in range(f...  10.3 us
    slice x16, local copies, waits for them, and re-layouts, advance(): towards[view, 0]  9.83 us
  transfers between devices with their start and end apart: 10, of which 3 were waited for; matrix products, arithmetic and copies ran while one was open for 6% of the time, Pallas kernels for 0%

commit v1 on v0

--- a/solution.py
+++ b/solution.py
@@ -1,11 +1,20 @@
+import functools
+import math
+
 import jax
 import jax.numpy as jnp
 from jax import lax
+from jax.experimental import pallas as pl
+from jax.experimental.pallas import tpu as pltpu
 from jax.sharding import PartitionSpec as P
 
 VIEWS = 4
 SHEAR = 8
 REACH = 32
+HALO = SHEAR + REACH
+SUB = 8
+LANES = 128
+MESH = pl.DeviceIdType.MESH
 
 
 def padded(cells, sides, width):
@@ -87,7 +96,7 @@
     return (ranks[:, None, :] < ranks[:, :, None]).astype(jnp.float32)
 
 
-def on_device(pressure, light, palette, rate, shear, offset, order):
+def many_bricks(pressure, light, palette, rate, shear, offset, order):
     depth_cells, rows, cols = pressure.shape
     brick = lax.axis_index("gz")
     zero = jnp.zeros((), jnp.int32)
@@ -122,9 +131,328 @@
     return image[:, :, None]
 
 
+def gather_cells(dims, p_ref, m_ref, l_ref, r_ref, lpk, rpk, sends, arrivals):
+    ny, nx, bz, rows = dims
+    strip = rows // 2
+    tall = HALO + strip + SUB
+    z, y, x = lax.axis_index("gz"), lax.axis_index("gy"), lax.axis_index("gx")
+    depth = 2 * bz
+
+    m_ref[0] = jnp.zeros((tall, LANES), jnp.float32)
+    m_ref[depth + 1] = jnp.zeros((tall, LANES), jnp.float32)
+    m_ref[:, :HALO] = jnp.zeros((depth + 2, HALO, LANES), jnp.float32)
+    m_ref[:, HALO + strip :] = jnp.zeros((depth + 2, SUB, LANES), jnp.float32)
+    l_ref[...] = jnp.zeros(l_ref.shape, jnp.float32)
+    r_ref[...] = jnp.zeros(r_ref.shape, jnp.float32)
+
+    has_up, has_down = y > 0, y < ny - 1
+    has_left, has_right = x > 0, x < nx - 1
+    cross = y + 2 * z - 1
+    has_cross = jnp.logical_and(cross >= 0, cross < ny)
+    always = y >= 0
+    partners = (
+        (always, (1 - z, y, x)),
+        (has_up, (z, y - 1, x)),
+        (has_down, (z, y + 1, x)),
+        (has_cross, (1 - z, cross, x)),
+        (has_left, (z, y, x - 1)),
+        (has_right, (z, y, x + 1)),
+    )
+    barrier = pltpu.get_barrier_semaphore()
+    for there, who in partners:
+
+        @pl.when(there)
+        def _():
+            pl.semaphore_signal(barrier, inc=1, device_id=who, device_id_type=MESH)
+
+    count = 1
+    for there, _ in partners[1:]:
+        count = count + there.astype(jnp.int32)
+    pl.semaphore_wait(barrier, count)
+
+    def remote(src, dst, slot, arrival, who):
+        return pltpu.make_async_remote_copy(
+            src_ref=src,
+            dst_ref=dst,
+            send_sem=sends.at[slot],
+            recv_sem=arrivals.at[arrival],
+            device_id=who,
+            device_id_type=MESH,
+        )
+
+    def planes(brick):
+        return pl.ds(1 + brick * bz, bz)
+
+    def copies(brick):
+        if brick == 0:
+            main = remote(
+                p_ref.at[:, strip - HALO :],
+                m_ref.at[planes(0), : HALO + strip],
+                0, 0, (1 - z, y, x),
+            )
+        else:
+            main = remote(
+                p_ref.at[:, : strip + SUB],
+                m_ref.at[planes(1), HALO:],
+                0, 0, (1 - z, y, x),
+            )
+        down = remote(
+            p_ref.at[:, rows - HALO :], m_ref.at[planes(brick), :HALO],
+            1, 1 + brick, (0, y + 1, x),
+        )
+        up = remote(
+            p_ref.at[:, :SUB], m_ref.at[planes(brick), HALO + strip :],
+            2, 1 + brick, (1, y - 1, x),
+        )
+        return main, down, up
+
+    for brick in range(2):
+
+        @pl.when(z == brick)
+        def _():
+            main, down, up = copies(brick)
+            main.start()
+
+            @pl.when(has_down)
+            def _():
+                down.start()
+
+            @pl.when(has_up)
+            def _():
+                up.start()
+
+            if brick == 0:
+                m_ref[planes(0), HALO:] = p_ref[:, : strip + SUB]
+            else:
+                m_ref[planes(1), : HALO + strip] = p_ref[:, strip - HALO :]
+
+    for brick in range(2):
+
+        @pl.when(z == brick)
+        def _():
+            main, down, up = copies(brick)
+            other_main, _, _ = copies(1 - brick)
+            other_main.wait_recv()
+            for source in range(2):
+                _, from_up, from_down = copies(source)
+                if brick == 0:
+
+                    @pl.when(has_up)
+                    def _():
+                        from_up.wait_recv()
+                else:
+
+                    @pl.when(has_down)
+                    def _():
+                        from_down.wait_recv()
+
+    lane = lax.broadcasted_iota(jnp.int32, (tall, LANES), 1)
+    per = LANES // HALO
+    first_lane = LANES - HALO
+    ends = jnp.zeros((tall, LANES), jnp.float32)
+    for group in range(l_ref.shape[0]):
+        packed = jnp.zeros((tall, LANES), jnp.float32)
+        for j in range(per):
+            k = group * per + j
+            if k < depth:
+                cells = m_ref[1 + k]
+                moved = pltpu.roll(cells, (j * HALO - first_lane) % LANES, 1)
+                packed = jnp.where(lane >= j * HALO, moved, packed)
+                ends = jnp.where(lane == k, pltpu.roll(cells, k, 1) if k else cells, ends)
+        lpk[group] = packed
+    rpk[...] = ends
+
+    rightward = remote(lpk, l_ref, 3, 3, (z, y, x + 1))
+    leftward = remote(rpk, r_ref, 4, 4, (z, y, x - 1))
+
+    @pl.when(has_right)
+    def _():
+        rightward.start()
+
+    @pl.when(has_left)
+    def _():
+        leftward.start()
+        rightward.wait_recv()
+
+    @pl.when(has_right)
+    def _():
+        leftward.wait_recv()
+
+    for brick in range(2):
+
+        @pl.when(z == brick)
+        def _():
+            main, down, up = copies(brick)
+            main.wait_send()
+
+            @pl.when(has_down)
+            def _():
+                down.wait_send()
+
+            @pl.when(has_up)
+            def _():
+                up.wait_send()
+
+    @pl.when(has_right)
+    def _():
+        rightward.wait_send()
+
+    @pl.when(has_left)
+    def _():
+        leftward.wait_send()
+
+
+def render_strip(
+    dims, light, palette, rate, shear, offset, order, m_ref, l_ref, r_ref, out_ref, h_ref, dm, dh
+):
+    ny, nx, bz, rows = dims
+    strip = rows // 2
+    tall = HALO + strip + SUB
+    depth = 2 * bz
+    per = LANES // HALO
+    first_lane = LANES - HALO
+    z, y, x = lax.axis_index("gz"), lax.axis_index("gy"), lax.axis_index("gx")
+
+    h_ref[0] = jnp.zeros((tall, LANES), jnp.float32)
+    h_ref[depth + 1] = jnp.zeros((tall, LANES), jnp.float32)
+    for k in range(depth):
+        shift = (first_lane - (k % per) * HALO) % LANES
+        h_ref[1 + k] = pltpu.roll(l_ref[k // per], shift, 1)
+
+    towards = []
+    for w in range(VIEWS):
+        a, b, c = light[w, 0], light[w, 1], light[w, 2]
+        inverse = lax.rsqrt(jnp.full((SUB, LANES), a * a + b * b + c * c + 1.0, jnp.float32))
+        towards.append((a * inverse, b * inverse, c * inverse))
+
+    lane = lax.broadcasted_iota(jnp.int32, (SUB, LANES), 1)
+    last = lane == LANES - 1
+    first = lane == 0
+
+    def slopes(k, carry):
+        for i in range((HALO + strip) // SUB):
+            top = i * SUB
+            here = m_ref[k + 1, top + 1 : top + 1 + SUB]
+            side = h_ref[k + 1, top + 1 : top + 1 + SUB]
+            beyond = pltpu.roll(r_ref[top + 1 : top + 1 + SUB], LANES - 1 - k, 1)
+            here_r, here_l = pltpu.roll(here, LANES - 1, 1), pltpu.roll(here, 1, 1)
+            side_r, side_l = pltpu.roll(side, LANES - 1, 1), pltpu.roll(side, 1, 1)
+            for ref, cols, dots in (
+                (m_ref, jnp.where(last, beyond, here_r) - jnp.where(first, side_l, here_l), dm),
+                (h_ref, jnp.where(last, here_r, side_r) - side_l, dh),
+            ):
+                deep = ref[k + 2, top + 1 : top + 1 + SUB] - ref[k, top + 1 : top + 1 + SUB]
+                down = ref[k + 1, top + 2 : top + 2 + SUB] - ref[k + 1, top : top + SUB]
+                half = 0.5 * lax.rsqrt(0.25 * (deep * deep + down * down + cols * cols) + 1.0)
+                deep, down, cols = deep * half, down * half, cols * half
+                for w in range(VIEWS):
+                    a, b, c = towards[w]
+                    dots[w, k, top : top + SUB] = deep * a + down * b + cols * c
+        return carry
+
+    lax.fori_loop(0, depth, slopes, 0)
+
+    tile = 32
+    base_row = y * rows + z * strip
+    base_col = x * LANES
+    lanes = lax.broadcasted_iota(jnp.int32, (tile, LANES), 1)
+    rows_at = lax.broadcasted_iota(jnp.int32, (tile, LANES), 0)
+    bias = [0.5 * palette[c, 0] for c in range(3)]
+    gain = [0.5 * palette[c, 1] for c in range(3)]
+
+    def view_part(step, carry):
+        w = step // (strip // tile)
+        top = (step % (strip // tile)) * tile
+        through = jnp.ones((tile, LANES), jnp.float32)
+        ambient = jnp.zeros((tile, LANES), jnp.float32)
+        colors = [jnp.zeros((tile, LANES), jnp.float32) for _ in range(3)]
+        rate2 = rate[w] * (-math.log2(math.e))
+        for place in range(2):
+            brick = order[w, place]
+            off_r, off_c = offset[w, brick, 0], offset[w, brick, 1]
+            inside = jnp.logical_and(
+                rows_at >= off_r - base_row - top, lanes >= off_c - base_col
+            )
+            fall = jnp.where(inside, rate2, 0.0)
+            for j in range(bz):
+                k = brick * bz + j
+                sr = off_r + shear[w, k, 0]
+                sc = off_c + shear[w, k, 1]
+                at = HALO + top - sr
+                wrap = lanes >= LANES - sc
+                value = jnp.where(
+                    wrap, h_ref[k + 1, pl.ds(at, tile)], m_ref[k + 1, pl.ds(at, tile)]
+                )
+                dot = jnp.where(wrap, dh[w, k, pl.ds(at - 1, tile)], dm[w, k, pl.ds(at - 1, tile)])
+                value = pltpu.roll(value, sc, 1)
+                dot = pltpu.roll(dot, sc, 1)
+                kept = jnp.exp2(fall * (1.0 + jnp.tanh(value)))
+                weight = (0.125 + 0.375 * dot * dot) * ((1.0 - kept) * through)
+                through = through * kept
+                ambient = ambient + weight
+                for c in range(3):
+                    colors[c] = colors[c] + weight * jnp.tanh(bias[c] + gain[c] * value)
+        for c in range(3):
+            out_ref[w, c, pl.ds(top, tile)] = ambient + colors[c]
+        out_ref[w, 3, pl.ds(top, tile)] = 1.0 - through
+        return carry
+
+    lax.fori_loop(0, VIEWS * (strip // tile), view_part, 0)
+
+
+def two_bricks(mesh, pressure, light, palette, rate, shear, offset, order):
+    bz, rows, cols = pressure.shape
+    dims = (mesh.shape["gy"], mesh.shape["gx"], bz, rows)
+    strip = rows // 2
+    tall = HALO + strip + SUB
+    depth = 2 * bz
+    groups = -(-depth // (LANES // HALO))
+    vmem = pl.BlockSpec(memory_space=pltpu.VMEM)
+    smem = pl.BlockSpec(memory_space=pltpu.SMEM)
+    f32 = jnp.float32
+    cells, left, right = pl.pallas_call(
+        functools.partial(gather_cells, dims),
+        out_shape=(
+            jax.ShapeDtypeStruct((depth + 2, tall, LANES), f32),
+            jax.ShapeDtypeStruct((groups, tall, LANES), f32),
+            jax.ShapeDtypeStruct((tall, LANES), f32),
+        ),
+        in_specs=[vmem],
+        out_specs=(vmem, vmem, vmem),
+        scratch_shapes=[
+            pltpu.VMEM((groups, tall, LANES), f32),
+            pltpu.VMEM((tall, LANES), f32),
+            pltpu.SemaphoreType.DMA((5,)),
+            pltpu.SemaphoreType.DMA((5,)),
+        ],
+        compiler_params=pltpu.CompilerParams(collective_id=0, has_side_effects=True),
+        name="gather_cells",
+    )(pressure)
+    image = pl.pallas_call(
+        functools.partial(render_strip, dims),
+        out_shape=jax.ShapeDtypeStruct((VIEWS, 4, strip, LANES), f32),
+        in_specs=[smem] * 6 + [vmem] * 3,
+        out_specs=vmem,
+        scratch_shapes=[
+            pltpu.VMEM((depth + 2, tall, LANES), f32),
+            pltpu.VMEM((VIEWS, depth, HALO + strip, LANES), f32),
+            pltpu.VMEM((VIEWS, depth, HALO + strip, LANES), f32),
+        ],
+        name="render_strip",
+    )(light, palette, rate, shear, offset, order, cells, left, right)
+    return image[:, :, None]
+
+
+def on_device(mesh, pressure, *rest):
+    bz, rows, cols = pressure.shape
+    if mesh.shape["gz"] == 2 and cols == LANES and rows % 64 == 0 and rows // 2 >= HALO:
+        return two_bricks(mesh, pressure, *rest)
+    return many_bricks(pressure, *rest)
+
+
 def solution(mesh):
     return jax.shard_map(
-        on_device,
+        functools.partial(on_device, mesh),
         mesh=mesh,
         in_specs=(P("gz", "gy", "gx"), P(), P(), P(), P(), P(), P()),
         out_specs=P(None, None, "gz", "gy", "gx"),

time: 230 us -> 25.2 us (0.11); the launches traced: 227 us -> 25 us
  other arithmetic: 65.6 us -> 0 us
  local copies, waits for them, and re-layouts: 55.3 us -> 3.43 us
  loops' own time: 39 us -> 0 us
  starting transfers between devices: 30.3 us -> 0 us
  Pallas kernels: 0 us -> 21.5 us
  waiting for transfers between devices: 20.5 us -> 0 us
  between operations: 15.4 us -> 0.01 us
    mul x34 -> x0, other arithmetic: 43 us -> none  [the longest x16 31 us: advance(): hues = jax.nn.sigmoid(offsets + slopes * value[None]) * shade[None]]
    another operation x4 -> x0, loops' own time: 39 us -> none  [render_layers(): lax.scan(advance, start_carry, (inner, normals[0], normals[1], normals[2]...]
    slice x51 -> x0, local copies, waits for them, and re-layouts: 32.2 us -> none  [the longest x16 9.83 us: advance(): towards[view, 0]]
    ppermute x9 -> x0, starting transfers between devices: 26.7 us -> none  [the longest x3 12.6 us: padded(): lax.ppermute(tail, axis, [(i, (i + 1) % count) for i in range(ends)])]
    pallas_call x0 -> x2, Pallas kernels: none -> 21.5 us  [the longest x1 16.1 us: two_bricks(): pl.pallas_call(functools.partial(gather_cells, dims), out_shape=(jax.Shap...]
    all_to_all x1 -> x0, waiting for transfers between devices: 13.7 us -> none  [on_device(): lax.all_to_all(own_tile[None], 'gz', split_axis=3, concat_axis=0, tiled=T...]
    add x33 -> x0, other arithmetic: 13.5 us -> none  [the longest x32 12 us: advance(): return ((color + hues * weight[None], depth + density), None)]
    dynamic_update_slice x4 -> x0, local copies, waits for them, and re-layouts: 10.8 us -> none  [on_device(): lax.dynamic_update_slice(blank, layers[view], (zero, moved[view, 0], move...]
  transfers between devices with their start and end apart: 10 -> 0, of which waited for: 3 -> 0; matrix products, arithmetic and copies ran while one was open for 6% -> 0% of each run, Pallas kernels for 0% -> 0%
where the time goes in v1:
time: 25.2 us; the launch traced here: 25 us
  Pallas kernels  21.5 us (85%)
  local copies, waits for them, and re-layouts  3.43 us (14%)
    pallas_call x1, Pallas kernels, two_bricks(): pl.pallas_call(functools.partial(gather_cells, dims), out_shape=(jax.Shap...  16.1 us
    pallas_call x1, Pallas kernels, two_bricks(): pl.pallas_call(functools.partial(render_strip, dims), out_shape=jax.Shape...  5.49 us
    unnamed x10, local copies, waits for them, and re-layouts  3.43 us

profile of v1, /device:TPU:0, one launch (start us, length us, event | category | flops | bytes accessed | tf_op | source)
XLA Modules:
  0.0 25.0 jit_solution(3214790919487195884)
XLA Ops:
  0.0 0.0 copy-start.2
  0.0 0.0 copy-start.1
  0.0 1.4 %copy.8.palette = f32[3,2]{1,0:T(4,128)} copy(f32[3,2]{0,1:T(2,128)} %param.9) | data formatting | bytes 48 | tf_op args[2]
  1.4 0.0 copy-done.2
  1.4 0.0 copy-start
  1.4 0.7 %copy.11.order = s32[4,2]{1,0:T(4,128)} copy(s32[4,2]{0,1:T(2,128)S(1)} %copy-done.2) | data formatting | bytes 64 | tf_op args[6]
  2.0 0.0 copy-done.1
  2.1 0.7 %copy.10.offset = s32[4,2,2]{2,1,0:T(2,128)} copy(s32[4,2,2]{0,2,1:T(2,128)S(1)} %copy-done.1) | data formatting | bytes 128 | tf_op args[5]
  2.7 0.0 copy-done
  2.7 0.7 %copy.9.shear = s32[4,8,2]{2,1,0:T(8,128)} copy(s32[4,8,2]{1,2,0:T(2,128)S(1)} %copy-done) | data formatting | bytes 512 | tf_op args[4]
  3.4 16.1 %gather_cells.1 = (f32[10,112,128]{2,1,0:T(8,128)}, f32[3,112,128]{2,1,0:T(8,128)}, f32[112,128]{1,0:T(8,128)}) custom-call(f32[4,128,128]{2,1,0:T(8,128)} %p_ref.1), custom_call_target="tpu_custom_call" | custom-call | tf_op jit(solution)/shard_map/gather_cells/pallas_call | solution.py:413
  19.5 5.5 %render_strip.1 = f32[4,4,64,128]{3,2,1,0:T(8,128)} custom-call(f32[4,3]{1,0:T(4,128)} %light.1, f32[3,2]{1,0:T(4,128)} %copy.8.palette, f32[4]{0:T(128)} %rate.1, s32[4,8,2]{2,1,0:T(8,128)} %copy.9.shear, s32[4,2,2]{2,1,0:T(2,128)} %copy.10.offset, s32[4,2]{1,0:T(4,128)} %copy.11.order, f32[10,112,128]{2,1,0:T(8,128)} %get-tuple-element.8.m_ref, ...), custom_call_target="tpu_custom_call" | custom-call | tf_op jit(solution)/shard_map/render_strip/pallas_call | solution.py:431
Async XLA Ops:
  0.0 1.4 %copy-start.2 = (s32[4,2]{0,1:T(2,128)S(1)}, s32[4,2]{0,1:T(2,128)}, u32[]{:S(2)}) copy-start(s32[4,2]{0,1:T(2,128)} %param.13) | copy-start | bytes 100
  0.0 2.0 %copy-start.1 = (s32[4,2,2]{0,2,1:T(2,128)S(1)}, s32[4,2,2]{0,2,1:T(2,128)}, u32[]{:S(2)}) copy-start(s32[4,2,2]{0,2,1:T(2,128)} %param.12) | copy-start | bytes 196
  1.4 1.4 %copy-start = (s32[4,8,2]{1,2,0:T(2,128)S(1)}, s32[4,8,2]{1,2,0:T(2,128)}, u32[]{:S(2)}) copy-start(s32[4,8,2]{1,2,0:T(2,128)} %param.11) | copy-start | bytes 772

commit v2 on v0

--- a/solution.py
+++ b/solution.py
@@ -1,11 +1,20 @@
+import functools
+import math
+
 import jax
 import jax.numpy as jnp
 from jax import lax
+from jax.experimental import pallas as pl
+from jax.experimental.pallas import tpu as pltpu
 from jax.sharding import PartitionSpec as P
 
 VIEWS = 4
 SHEAR = 8
 REACH = 32
+HALO = SHEAR + REACH
+SUB = 8
+LANES = 128
+MESH = pl.DeviceIdType.MESH
 
 
 def padded(cells, sides, width):
@@ -87,7 +96,7 @@
     return (ranks[:, None, :] < ranks[:, :, None]).astype(jnp.float32)
 
 
-def on_device(pressure, light, palette, rate, shear, offset, order):
+def many_bricks(pressure, light, palette, rate, shear, offset, order):
     depth_cells, rows, cols = pressure.shape
     brick = lax.axis_index("gz")
     zero = jnp.zeros((), jnp.int32)
@@ -122,9 +131,367 @@
     return image[:, :, None]
 
 
+def exchange(dims, mine, here, p_ref, m_ref, l_ref, r_ref, lpk, rpk, sends, arrivals, local_sem):
+    ny, nx, bz, rows = dims
+    z, y, x = here
+    strip = rows // 2
+    tall = HALO + strip + SUB
+    per = LANES // HALO
+    groups = -(-bz // per)
+    other = 1 - mine
+    first_lane = LANES - HALO
+    has_up, has_down = y > 0, y < ny - 1
+    has_left, has_right = x > 0, x < nx - 1
+
+    def remote(src, dst, slot, arrival, who):
+        return pltpu.make_async_remote_copy(
+            src_ref=src,
+            dst_ref=dst,
+            send_sem=sends.at[slot],
+            recv_sem=arrivals.at[arrival],
+            device_id=who,
+            device_id_type=MESH,
+        )
+
+    def spans(to):
+        if to == 0:
+            return pl.ds(0, strip + SUB), pl.ds(HALO, strip + SUB)
+        return pl.ds(strip - HALO, HALO + strip), pl.ds(0, HALO + strip)
+
+    def main(brick, g):
+        count = min(per, bz - g * per)
+        source, target = spans(1 - brick)
+        return remote(
+            p_ref.at[pl.ds(g * per, count), source],
+            m_ref.at[pl.ds(1 + brick * bz + g * per, count), target],
+            g, g, (1 - z, y, x),
+        )
+
+    def down(brick):
+        return remote(
+            p_ref.at[:, pl.ds(rows - HALO, HALO)],
+            m_ref.at[pl.ds(1 + brick * bz, bz), pl.ds(0, HALO)],
+            groups, groups + brick, (0, y + 1, x),
+        )
+
+    def up(brick):
+        return remote(
+            p_ref.at[:, pl.ds(0, SUB)],
+            m_ref.at[pl.ds(1 + brick * bz, bz), pl.ds(HALO + strip, SUB)],
+            groups + 1, groups + brick, (1, y - 1, x),
+        )
+
+    def rightward(brick, g):
+        slot = groups + 2 + brick * groups + g
+        return remote(
+            lpk.at[brick * groups + g], l_ref.at[brick * groups + g], slot, slot, (z, y, x + 1)
+        )
+
+    def leftward(brick):
+        slot = 3 * groups + 2 + brick
+        return remote(rpk.at[brick], r_ref.at[brick], slot, slot, (z, y, x - 1))
+
+    def started(there, copy):
+        @pl.when(there)
+        def _():
+            copy.start()
+
+    def arrived(there, copy):
+        @pl.when(there)
+        def _():
+            copy.wait_recv()
+
+    def left(there, copy):
+        @pl.when(there)
+        def _():
+            copy.wait_send()
+
+    lane = lax.broadcasted_iota(jnp.int32, (tall, LANES), 1)
+
+    def pack(brick, g):
+        packed = jnp.zeros((tall, LANES), jnp.float32)
+        for j in range(min(per, bz - g * per)):
+            cells = m_ref[1 + brick * bz + g * per + j]
+            moved = pltpu.roll(cells, (j * HALO - first_lane) % LANES, 1)
+            packed = jnp.where(lane >= j * HALO, moved, packed)
+        lpk[brick * groups + g] = packed
+
+    def pack_ends(brick):
+        ends = jnp.zeros((tall, LANES), jnp.float32)
+        for j in range(bz):
+            cells = m_ref[1 + brick * bz + j]
+            ends = jnp.where(lane == j, pltpu.roll(cells, j, 1) if j else cells, ends)
+        rpk[brick] = ends
+
+    def halo_in(brick):
+        if mine == 0:
+            arrived(has_up, down(brick))
+        else:
+            arrived(has_down, up(brick))
+
+    def open_up():
+        source, target = spans(mine)
+        own = pltpu.make_async_copy(
+            p_ref.at[:, source], m_ref.at[pl.ds(1 + mine * bz, bz), target], local_sem
+        )
+        started(has_down, down(mine))
+        started(has_up, up(mine))
+        for g in range(groups):
+            main(mine, g).start()
+        own.start()
+        own.wait()
+        halo_in(mine)
+        for g in range(groups):
+            pack(mine, g)
+            started(has_right, rightward(mine, g))
+        pack_ends(mine)
+        started(has_left, leftward(mine))
+        halo_in(other)
+        for g in range(groups):
+            main(other, g).wait_recv()
+            pack(other, g)
+            started(has_right, rightward(other, g))
+        pack_ends(other)
+        started(has_left, leftward(other))
+
+    def columns_in(brick):
+        for g in range(groups):
+            arrived(has_left, rightward(brick, g))
+        arrived(has_right, leftward(brick))
+
+    def close():
+        for g in range(groups):
+            main(mine, g).wait_send()
+        left(has_down, down(mine))
+        left(has_up, up(mine))
+        for brick in range(2):
+            for g in range(groups):
+                left(has_right, rightward(brick, g))
+            left(has_left, leftward(brick))
+
+    return open_up, columns_in, close
+
+
+def render(
+    dims, light, palette, rate, shear, offset, order, p_ref, out_ref,
+    m_ref, l_ref, r_ref, lpk, rpk, h_ref, dm, dh, sends, arrivals, local_sem,
+):
+    ny, nx, bz, rows = dims
+    strip = rows // 2
+    tall = HALO + strip + SUB
+    depth = 2 * bz
+    per = LANES // HALO
+    groups = -(-bz // per)
+    first_lane = LANES - HALO
+    z, y, x = lax.axis_index("gz"), lax.axis_index("gy"), lax.axis_index("gx")
+    has_up, has_down = y > 0, y < ny - 1
+    has_left, has_right = x > 0, x < nx - 1
+
+    empty = jnp.zeros((tall, LANES), jnp.float32)
+    for ref in (m_ref, h_ref):
+        ref[0] = empty
+        ref[depth + 1] = empty
+
+    @pl.when(jnp.logical_and(z == 0, y == 0))
+    def _():
+        m_ref[:, :HALO] = jnp.zeros((depth + 2, HALO, LANES), jnp.float32)
+
+    @pl.when(jnp.logical_and(z == 1, y == ny - 1))
+    def _():
+        m_ref[:, HALO + strip :] = jnp.zeros((depth + 2, SUB, LANES), jnp.float32)
+
+    @pl.when(x == 0)
+    def _():
+        l_ref[...] = jnp.zeros(l_ref.shape, jnp.float32)
+
+    @pl.when(x == nx - 1)
+    def _():
+        r_ref[...] = jnp.zeros(r_ref.shape, jnp.float32)
+
+    cross = y + 2 * z - 1
+    partners = (
+        (y >= 0, (1 - z, y, x)),
+        (has_up, (z, y - 1, x)),
+        (has_down, (z, y + 1, x)),
+        (jnp.logical_and(cross >= 0, cross < ny), (1 - z, cross, x)),
+        (has_left, (z, y, x - 1)),
+        (has_right, (z, y, x + 1)),
+    )
+    barrier = pltpu.get_barrier_semaphore()
+    count = 0
+    for there, who in partners:
+
+        @pl.when(there)
+        def _():
+            pl.semaphore_signal(barrier, inc=1, device_id=who, device_id_type=MESH)
+
+        count = count + there.astype(jnp.int32)
+    pl.semaphore_wait(barrier, count)
+
+    steps = [
+        exchange(
+            dims, mine, (z, y, x), p_ref, m_ref, l_ref, r_ref, lpk, rpk, sends, arrivals, local_sem
+        )
+        for mine in range(2)
+    ]
+
+    for mine in range(2):
+
+        @pl.when(z == mine)
+        def _():
+            steps[mine][0]()
+            steps[mine][1](mine)
+
+    def unpack(brick):
+        for j in range(bz):
+            shift = (first_lane - (j % per) * HALO) % LANES
+            h_ref[1 + brick * bz + j] = pltpu.roll(l_ref[brick * groups + j // per], shift, 1)
+
+    towards = []
+    for w in range(VIEWS):
+        a, b, c = light[w, 0], light[w, 1], light[w, 2]
+        inverse = lax.rsqrt(jnp.full((SUB, LANES), a * a + b * b + c * c + 1.0, jnp.float32))
+        towards.append((a * inverse, b * inverse, c * inverse))
+
+    lane = lax.broadcasted_iota(jnp.int32, (SUB, LANES), 1)
+    last = lane == LANES - 1
+    first = lane == 0
+
+    def slopes(k, carry):
+        for i in range((HALO + strip) // SUB):
+            top = i * SUB
+            here = m_ref[k + 1, top + 1 : top + 1 + SUB]
+            side = h_ref[k + 1, top + 1 : top + 1 + SUB]
+            beyond = pltpu.roll(r_ref[k // bz, top + 1 : top + 1 + SUB], LANES - 1 - k % bz, 1)
+            here_r, here_l = pltpu.roll(here, LANES - 1, 1), pltpu.roll(here, 1, 1)
+            side_r, side_l = pltpu.roll(side, LANES - 1, 1), pltpu.roll(side, 1, 1)
+            for ref, cols, dots in (
+                (m_ref, jnp.where(last, beyond, here_r) - jnp.where(first, side_l, here_l), dm),
+                (h_ref, jnp.where(last, here_r, side_r) - side_l, dh),
+            ):
+                deep = ref[k + 2, top + 1 : top + 1 + SUB] - ref[k, top + 1 : top + 1 + SUB]
+                down = ref[k + 1, top + 2 : top + 2 + SUB] - ref[k + 1, top : top + SUB]
+                half = 0.5 * lax.rsqrt(0.25 * (deep * deep + down * down + cols * cols) + 1.0)
+                deep, down, cols = deep * half, down * half, cols * half
+                for w in range(VIEWS):
+                    a, b, c = towards[w]
+                    dots[w, k, top : top + SUB] = deep * a + down * b + cols * c
+        return carry
+
+    unpack(z)
+    lax.fori_loop(z * (bz + 1), z * (bz + 1) + bz - 1, slopes, 0)
+
+    for mine in range(2):
+
+        @pl.when(z == mine)
+        def _():
+            steps[mine][1](1 - mine)
+            steps[mine][2]()
+
+    unpack(1 - z)
+    lax.fori_loop((1 - z) * (bz - 1), (1 - z) * (bz - 1) + bz + 1, slopes, 0)
+
+    tile = 32
+    base_row = y * rows + z * strip
+    base_col = x * LANES
+    lanes = lax.broadcasted_iota(jnp.int32, (tile, LANES), 1)
+    rows_at = lax.broadcasted_iota(jnp.int32, (tile, LANES), 0)
+    bias = [0.5 * palette[0, c] for c in range(3)]
+    gain = [0.5 * palette[1, c] for c in range(3)]
+
+    def view_part(step, carry):
+        w = step // (strip // tile)
+        top = (step % (strip // tile)) * tile
+        through = jnp.ones((tile, LANES), jnp.float32)
+        ambient = jnp.zeros((tile, LANES), jnp.float32)
+        colors = [jnp.zeros((tile, LANES), jnp.float32) for _ in range(3)]
+        rate2 = rate[w] * (-math.log2(math.e))
+        for place in range(2):
+            brick = order[place, w]
+            off_r, off_c = offset[brick, 0, w], offset[brick, 1, w]
+            inside = jnp.logical_and(
+                rows_at >= off_r - base_row - top, lanes >= off_c - base_col
+            )
+            fall = jnp.where(inside, rate2, 0.0)
+            for j in range(bz):
+                k = brick * bz + j
+                sr = off_r + shear[w, 0, k]
+                sc = off_c + shear[w, 1, k]
+                at = HALO + top - sr
+                wrap = lanes >= LANES - sc
+                value = jnp.where(
+                    wrap, h_ref[k + 1, pl.ds(at, tile)], m_ref[k + 1, pl.ds(at, tile)]
+                )
+                dot = jnp.where(wrap, dh[w, k, pl.ds(at - 1, tile)], dm[w, k, pl.ds(at - 1, tile)])
+                value = pltpu.roll(value, sc, 1)
+                dot = pltpu.roll(dot, sc, 1)
+                kept = jnp.exp2(fall * (1.0 + jnp.tanh(value)))
+                weight = (0.125 + 0.375 * dot * dot) * ((1.0 - kept) * through)
+                through = through * kept
+                ambient = ambient + weight
+                for c in range(3):
+                    colors[c] = colors[c] + weight * jnp.tanh(bias[c] + gain[c] * value)
+        for c in range(3):
+            out_ref[w, c, pl.ds(top, tile)] = ambient + colors[c]
+        out_ref[w, 3, pl.ds(top, tile)] = 1.0 - through
+        return carry
+
+    lax.fori_loop(0, VIEWS * (strip // tile), view_part, 0)
+
+
+def two_bricks(mesh, pressure, light, palette, rate, shear, offset, order):
+    bz, rows, cols = pressure.shape
+    dims = (mesh.shape["gy"], mesh.shape["gx"], bz, rows)
+    strip = rows // 2
+    tall = HALO + strip + SUB
+    depth = 2 * bz
+    groups = -(-bz // (LANES // HALO))
+    vmem = pl.BlockSpec(memory_space=pltpu.VMEM)
+    smem = pl.BlockSpec(memory_space=pltpu.SMEM)
+    f32 = jnp.float32
+    copies = 3 * groups + 4
+    image = pl.pallas_call(
+        functools.partial(render, dims),
+        out_shape=jax.ShapeDtypeStruct((VIEWS, 4, strip, LANES), f32),
+        in_specs=[smem] * 6 + [pl.BlockSpec(memory_space=pl.ANY)],
+        out_specs=vmem,
+        scratch_shapes=[
+            pltpu.VMEM((depth + 2, tall, LANES), f32),
+            pltpu.VMEM((2 * groups, tall, LANES), f32),
+            pltpu.VMEM((2, tall, LANES), f32),
+            pltpu.VMEM((2 * groups, tall, LANES), f32),
+            pltpu.VMEM((2, tall, LANES), f32),
+            pltpu.VMEM((depth + 2, tall, LANES), f32),
+            pltpu.VMEM((VIEWS, depth, HALO + strip, LANES), f32),
+            pltpu.VMEM((VIEWS, depth, HALO + strip, LANES), f32),
+            pltpu.SemaphoreType.DMA((copies,)),
+            pltpu.SemaphoreType.DMA((copies,)),
+            pltpu.SemaphoreType.DMA,
+        ],
+        compiler_params=pltpu.CompilerParams(collective_id=0, has_side_effects=True),
+        name="render",
+    )(
+        light,
+        palette.T,
+        rate,
+        jnp.transpose(shear, (0, 2, 1)),
+        jnp.transpose(offset, (1, 2, 0)),
+        order.T,
+        pressure,
+    )
+    return image[:, :, None]
+
+
+def on_device(mesh, pressure, *rest):
+    bz, rows, cols = pressure.shape
+    if mesh.shape["gz"] == 2 and cols == LANES and rows % 64 == 0 and rows // 2 >= HALO:
+        return two_bricks(mesh, pressure, *rest)
+    return many_bricks(pressure, *rest)
+
+
 def solution(mesh):
     return jax.shard_map(
-        on_device,
+        functools.partial(on_device, mesh),
         mesh=mesh,
         in_specs=(P("gz", "gy", "gx"), P(), P(), P(), P(), P(), P()),
         out_specs=P(None, None, "gz", "gy", "gx"),

time: 230 us -> 21.3 us (0.09); the launches traced: 227 us -> 21.1 us
  other arithmetic: 65.6 us -> 0 us
  local copies, waits for them, and re-layouts: 55.3 us -> 1.89 us
  loops' own time: 39 us -> 0 us
  starting transfers between devices: 30.3 us -> 0 us
  waiting for transfers between devices: 20.5 us -> 0 us
  Pallas kernels: 0 us -> 19.2 us
  between operations: 15.4 us -> 0.01 us
    mul x34 -> x0, other arithmetic: 43 us -> none  [the longest x16 31 us: advance(): hues = jax.nn.sigmoid(offsets + slopes * value[None]) * shade[None]]
    another operation x4 -> x0, loops' own time: 39 us -> none  [render_layers(): lax.scan(advance, start_carry, (inner, normals[0], normals[1], normals[2]...]
    slice x51 -> x0, local copies, waits for them, and re-layouts: 32.2 us -> none  [the longest x16 9.83 us: advance(): towards[view, 0]]
    ppermute x9 -> x0, starting transfers between devices: 26.7 us -> none  [the longest x3 12.6 us: padded(): lax.ppermute(tail, axis, [(i, (i + 1) % count) for i in range(ends)])]
    pallas_call x0 -> x1, Pallas kernels: none -> 19.2 us  [two_bricks(): pl.pallas_call(functools.partial(render, dims), out_shape=jax.ShapeDtypeS...]
    all_to_all x1 -> x0, waiting for transfers between devices: 13.7 us -> none  [on_device(): lax.all_to_all(own_tile[None], 'gz', split_axis=3, concat_axis=0, tiled=T...]
    add x33 -> x0, other arithmetic: 13.5 us -> none  [the longest x32 12 us: advance(): return ((color + hues * weight[None], depth + density), None)]
    dynamic_update_slice x4 -> x0, local copies, waits for them, and re-layouts: 10.8 us -> none  [on_device(): lax.dynamic_update_slice(blank, layers[view], (zero, moved[view, 0], move...]
  transfers between devices with their start and end apart: 10 -> 0, of which waited for: 3 -> 0; matrix products, arithmetic and copies ran while one was open for 6% -> 0% of each run, Pallas kernels for 0% -> 0%
where the time goes in v2:
time: 21.3 us; the launch traced here: 21.1 us
  Pallas kernels  19.2 us (90%)
  local copies, waits for them, and re-layouts  1.89 us (9%)
    pallas_call x1, Pallas kernels, two_bricks(): pl.pallas_call(functools.partial(render, dims), out_shape=jax.ShapeDtypeS...  19.2 us
    unnamed x1, local copies, waits for them, and re-layouts  1.89 us

profile of v2, /device:TPU:0, one launch (start us, length us, event | category | flops | bytes accessed | tf_op | source)
XLA Modules:
  0.0 21.1 jit_solution(3400825746179065394)
XLA Ops:
  0.0 19.2 %render.1 = f32[4,4,64,128]{3,2,1,0:T(8,128)} custom-call(f32[4,3]{1,0:T(4,128)} %light.1, f32[2,3]{1,0:T(2,128)} %bitcast.10, f32[4]{0:T(128)} %rate.1, s32[4,2,8]{2,1,0:T(2,128)} %bitcast.8, s32[2,2,4]{2,1,0:T(2,128)} %bitcast.9, s32[2,4]{1,0:T(2,128)} %bitcast.11, f32[4,128,128]{2,1,0:T(8,128)} %p_ref.1), custom_call_target="tpu_custom_call" | custom-call | tf_op jit(solution)/shard_map/render/pallas_call | solution.py:453
  19.2 1.9 %copy.10 = f32[4,4,1,64,128]{4,3,2,1,0:T(8,128)} copy(f32[4,4,1,64,128]{4,3,2,1,0:T(8,128)} %bitcast.7) | data formatting | bytes 1048576

commit v3 on v2

--- a/solution.py
+++ b/solution.py
@@ -13,6 +13,7 @@
 REACH = 32
 HALO = SHEAR + REACH
 SUB = 8
+BLOCK = 16
 LANES = 128
 MESH = pl.DeviceIdType.MESH
 
@@ -131,7 +132,14 @@
     return image[:, :, None]
 
 
-def exchange(dims, mine, here, p_ref, m_ref, l_ref, r_ref, lpk, rpk, sends, arrivals, local_sem):
+def segments(tall):
+    return (0, HALO, tall - HALO)
+
+
+def exchange(
+    dims, mine, here, p_ref, m_ref, full_in, rest_in, ends_in, full_out, rest_out, ends_out, sends,
+    arrivals, local_sem,
+):
     ny, nx, bz, rows = dims
     z, y, x = here
     strip = rows // 2
@@ -183,13 +191,14 @@
 
     def rightward(brick, g):
         slot = groups + 2 + brick * groups + g
-        return remote(
-            lpk.at[brick * groups + g], l_ref.at[brick * groups + g], slot, slot, (z, y, x + 1)
-        )
+        if g == groups - 1:
+            return remote(rest_out.at[brick], rest_in.at[brick], slot, slot, (z, y, x + 1))
+        at = brick * (groups - 1) + g
+        return remote(full_out.at[at], full_in.at[at], slot, slot, (z, y, x + 1))
 
     def leftward(brick):
         slot = 3 * groups + 2 + brick
-        return remote(rpk.at[brick], r_ref.at[brick], slot, slot, (z, y, x - 1))
+        return remote(ends_out.at[brick], ends_in.at[brick], slot, slot, (z, y, x - 1))
 
     def started(there, copy):
         @pl.when(there)
@@ -206,22 +215,31 @@
         def _():
             copy.wait_send()
 
-    lane = lax.broadcasted_iota(jnp.int32, (tall, LANES), 1)
-
     def pack(brick, g):
-        packed = jnp.zeros((tall, LANES), jnp.float32)
-        for j in range(min(per, bz - g * per)):
-            cells = m_ref[1 + brick * bz + g * per + j]
-            moved = pltpu.roll(cells, (j * HALO - first_lane) % LANES, 1)
+        if g == groups - 1:
+            lane = lax.broadcasted_iota(jnp.int32, (HALO, LANES), 1)
+            pieces = [m_ref[brick * bz + bz, row : row + HALO] for row in segments(tall)]
+        else:
+            lane = lax.broadcasted_iota(jnp.int32, (tall, LANES), 1)
+            pieces = [m_ref[1 + brick * bz + g * per + j] for j in range(per)]
+        packed = pltpu.roll(pieces[0], LANES - first_lane, 1)
+        for j in range(1, per):
+            moved = pltpu.roll(pieces[j], (j * HALO - first_lane) % LANES, 1)
             packed = jnp.where(lane >= j * HALO, moved, packed)
-        lpk[brick * groups + g] = packed
+        if g == groups - 1:
+            rest_out[brick] = packed
+        else:
+            full_out[brick * (groups - 1) + g] = packed
 
     def pack_ends(brick):
-        ends = jnp.zeros((tall, LANES), jnp.float32)
+        lane = lax.broadcasted_iota(jnp.int32, (BLOCK, LANES), 1)
+        ends = jnp.zeros((BLOCK, LANES), jnp.float32)
         for j in range(bz):
-            cells = m_ref[1 + brick * bz + j]
-            ends = jnp.where(lane == j, pltpu.roll(cells, j, 1) if j else cells, ends)
-        rpk[brick] = ends
+            for i in range(tall // BLOCK):
+                at = i * bz + j
+                cells = m_ref[1 + brick * bz + j, i * BLOCK : (i + 1) * BLOCK]
+                ends = jnp.where(lane == at, pltpu.roll(cells, at, 1) if at else cells, ends)
+        ends_out[brick] = ends
 
     def halo_in(brick):
         if mine == 0:
@@ -273,8 +291,9 @@
 
 
 def render(
-    dims, light, palette, rate, shear, offset, order, p_ref, out_ref,
-    m_ref, l_ref, r_ref, lpk, rpk, h_ref, dm, dh, sends, arrivals, local_sem,
+    dims, light_in, palette_in, rate_in, shear_in, offset_in, order_in, p_ref, out_ref,
+    light, palette, rate, shear, offset, order, m_ref, full_in, rest_in, ends_in,
+    full_out, rest_out, ends_out, h_ref, r_ref, dm, dh, sends, arrivals, local_sem, table_sems,
 ):
     ny, nx, bz, rows = dims
     strip = rows // 2
@@ -287,6 +306,18 @@
     has_up, has_down = y > 0, y < ny - 1
     has_left, has_right = x > 0, x < nx - 1
 
+    tables = [
+        pltpu.make_async_copy(source, target, table_sems.at[i])
+        for i, (source, target) in enumerate(
+            (
+                (light_in, light), (palette_in, palette), (rate_in, rate),
+                (shear_in, shear), (offset_in, offset), (order_in, order),
+            )
+        )
+    ]
+    for copy in tables:
+        copy.start()
+
     empty = jnp.zeros((tall, LANES), jnp.float32)
     for ref in (m_ref, h_ref):
         ref[0] = empty
@@ -302,11 +333,12 @@
 
     @pl.when(x == 0)
     def _():
-        l_ref[...] = jnp.zeros(l_ref.shape, jnp.float32)
+        full_in[...] = jnp.zeros(full_in.shape, jnp.float32)
+        rest_in[...] = jnp.zeros(rest_in.shape, jnp.float32)
 
     @pl.when(x == nx - 1)
     def _():
-        r_ref[...] = jnp.zeros(r_ref.shape, jnp.float32)
+        ends_in[...] = jnp.zeros(ends_in.shape, jnp.float32)
 
     cross = y + 2 * z - 1
     partners = (
@@ -330,7 +362,8 @@
 
     steps = [
         exchange(
-            dims, mine, (z, y, x), p_ref, m_ref, l_ref, r_ref, lpk, rpk, sends, arrivals, local_sem
+            dims, mine, (z, y, x), p_ref, m_ref, full_in, rest_in, ends_in, full_out, rest_out,
+            ends_out, sends, arrivals, local_sem,
         )
         for mine in range(2)
     ]
@@ -343,9 +376,21 @@
             steps[mine][1](mine)
 
     def unpack(brick):
-        for j in range(bz):
+        for j in range(bz - 1):
             shift = (first_lane - (j % per) * HALO) % LANES
-            h_ref[1 + brick * bz + j] = pltpu.roll(l_ref[brick * groups + j // per], shift, 1)
+            cells = full_in[brick * (groups - 1) + j // per]
+            h_ref[1 + brick * bz + j] = pltpu.roll(cells, shift, 1)
+        cells = rest_in[brick]
+        for j, row in enumerate(segments(tall)):
+            moved = pltpu.roll(cells, (first_lane - j * HALO) % LANES, 1)
+            h_ref[brick * bz + bz, row : row + HALO] = moved
+        cells = ends_in[brick]
+        for i in range(tall // BLOCK):
+            moved = pltpu.roll(cells, (LANES - 1 - i * bz) % LANES, 1)
+            r_ref[brick, i * BLOCK : (i + 1) * BLOCK] = moved
+
+    for copy in tables:
+        copy.wait()
 
     towards = []
     for w in range(VIEWS):
@@ -362,7 +407,9 @@
             top = i * SUB
             here = m_ref[k + 1, top + 1 : top + 1 + SUB]
             side = h_ref[k + 1, top + 1 : top + 1 + SUB]
-            beyond = pltpu.roll(r_ref[k // bz, top + 1 : top + 1 + SUB], LANES - 1 - k % bz, 1)
+            beyond = pltpu.roll(
+                r_ref[k // bz, top + 1 : top + 1 + SUB], (LANES - k % bz) % LANES, 1
+            )
             here_r, here_l = pltpu.roll(here, LANES - 1, 1), pltpu.roll(here, 1, 1)
             side_r, side_l = pltpu.roll(side, LANES - 1, 1), pltpu.roll(side, 1, 1)
             for ref, cols, dots in (
@@ -447,44 +494,64 @@
     depth = 2 * bz
     groups = -(-bz // (LANES // HALO))
     vmem = pl.BlockSpec(memory_space=pltpu.VMEM)
-    smem = pl.BlockSpec(memory_space=pltpu.SMEM)
+    hbm = pl.BlockSpec(memory_space=pltpu.HBM)
     f32 = jnp.float32
     copies = 3 * groups + 4
-    image = pl.pallas_call(
-        functools.partial(render, dims),
-        out_shape=jax.ShapeDtypeStruct((VIEWS, 4, strip, LANES), f32),
-        in_specs=[smem] * 6 + [pl.BlockSpec(memory_space=pl.ANY)],
-        out_specs=vmem,
-        scratch_shapes=[
-            pltpu.VMEM((depth + 2, tall, LANES), f32),
-            pltpu.VMEM((2 * groups, tall, LANES), f32),
-            pltpu.VMEM((2, tall, LANES), f32),
-            pltpu.VMEM((2 * groups, tall, LANES), f32),
-            pltpu.VMEM((2, tall, LANES), f32),
-            pltpu.VMEM((depth + 2, tall, LANES), f32),
-            pltpu.VMEM((VIEWS, depth, HALO + strip, LANES), f32),
-            pltpu.VMEM((VIEWS, depth, HALO + strip, LANES), f32),
-            pltpu.SemaphoreType.DMA((copies,)),
-            pltpu.SemaphoreType.DMA((copies,)),
-            pltpu.SemaphoreType.DMA,
-        ],
-        compiler_params=pltpu.CompilerParams(collective_id=0, has_side_effects=True),
-        name="render",
-    )(
+    tables = (
         light,
         palette.T,
         rate,
         jnp.transpose(shear, (0, 2, 1)),
         jnp.transpose(offset, (1, 2, 0)),
         order.T,
-        pressure,
+    )
+    image = pl.pallas_call(
+        functools.partial(render, dims),
+        out_shape=jax.ShapeDtypeStruct((VIEWS, 4, strip, LANES), f32),
+        in_specs=[hbm] * 7,
+        out_specs=vmem,
+        scratch_shapes=[
+            *[pltpu.SMEM(table.shape, table.dtype) for table in tables],
+            pltpu.VMEM((depth + 2, tall, LANES), f32),
+            pltpu.VMEM((2 * groups - 2, tall, LANES), f32),
+            pltpu.VMEM((2, HALO, LANES), f32),
+            pltpu.VMEM((2, BLOCK, LANES), f32),
+            pltpu.VMEM((2 * groups - 2, tall, LANES), f32),
+            pltpu.VMEM((2, HALO, LANES), f32),
+            pltpu.VMEM((2, BLOCK, LANES), f32),
+            pltpu.VMEM((depth + 2, tall, LANES), f32),
+            pltpu.VMEM((2, tall, LANES), f32),
+            pltpu.VMEM((VIEWS, depth, HALO + strip, LANES), f32),
+            pltpu.VMEM((VIEWS, depth, HALO + strip, LANES), f32),
+            pltpu.SemaphoreType.DMA((copies,)),
+            pltpu.SemaphoreType.DMA((copies,)),
+            pltpu.SemaphoreType.DMA,
+            pltpu.SemaphoreType.DMA((len(tables),)),
+        ],
+        compiler_params=pltpu.CompilerParams(collective_id=0, has_side_effects=True, vmem_limit_bytes=12 << 20),
+        name="render",
+    )(
+        *[pltpu.with_memory_space_constraint(t, pltpu.HBM) for t in (*tables, pressure)]
     )
     return image[:, :, None]
 
 
+def fits(mesh, shape):
+    bz, rows, cols = shape
+    tall = HALO + rows // 2 + SUB
+    return (
+        mesh.shape["gz"] == 2
+        and cols == LANES
+        and rows % 64 == 0
+        and 2 * HALO <= tall <= 3 * HALO
+        and tall % BLOCK == 0
+        and bz % (LANES // HALO) == 1
+        and bz * (tall // BLOCK) <= LANES
+    )
+
+
 def on_device(mesh, pressure, *rest):
-    bz, rows, cols = pressure.shape
-    if mesh.shape["gz"] == 2 and cols == LANES and rows % 64 == 0 and rows // 2 >= HALO:
+    if fits(mesh, pressure.shape):
         return two_bricks(mesh, pressure, *rest)
     return many_bricks(pressure, *rest)
 

time: 21.3 us -> 18.1 us (0.85)
  Pallas kernels: 19.2 us -> 17.1 us
  local copies, waits for them, and re-layouts: 1.89 us -> 0.8 us
    pallas_call x1, Pallas kernels: 19.2 us -> 17.1 us  [two_bricks(): pl.pallas_call(functools.partial(render, dims), out_shape=jax.ShapeDtypeS...]
    unnamed x1, local copies, waits for them, and re-layouts: 1.89 us -> 0.8 us
where the time goes in v3:
time: 18.1 us; the launch traced here: 17.9 us
  Pallas kernels  17.1 us (94%)
  local copies, waits for them, and re-layouts  0.8 us (4%)
    pallas_call x1, Pallas kernels, two_bricks(): pl.pallas_call(functools.partial(render, dims), out_shape=jax.ShapeDtypeS...  17.1 us
    unnamed x1, local copies, waits for them, and re-layouts  0.8 us

profile of v3, /device:TPU:0, one launch (start us, length us, event | category | flops | bytes accessed | tf_op | source)
XLA Modules:
  0.0 17.9 jit_solution(5068556944065398079)
XLA Ops:
  0.0 17.1 %render.1 = f32[4,4,64,128]{3,2,1,0:T(8,128)S(1)} custom-call(f32[4,3]{1,0:T(4,128)} %light_in.1, f32[2,3]{1,0:T(2,128)} %bitcast.10, f32[4]{0:T(128)} %rate_in.1, s32[4,2,8]{2,1,0:T(2,128)} %bitcast.8, s32[2,2,4]{2,1,0:T(2,128)} %bitcast.9, s32[2,4]{1,0:T(2,128)} %bitcast.11, f32[4,128,128]{2,1,0:T(8,128)} %p_ref.1), custom_call_target="tpu_custom_call" | custom-call | tf_op jit(solution)/shard_map/render/pallas_call | solution.py:508
  17.1 0.8 %copy.10 = f32[4,4,1,64,128]{4,3,2,1,0:T(8,128)} copy(f32[4,4,1,64,128]{4,3,2,1,0:T(8,128)S(1)} %bitcast.7) | data formatting | bytes 1048576

commit v4 on v3

--- a/solution.py
+++ b/solution.py
@@ -247,17 +247,18 @@
         else:
             arrived(has_down, up(brick))
 
+    def own():
+        source, target = spans(mine)
+        return pltpu.make_async_copy(
+            p_ref.at[:, source], m_ref.at[pl.ds(1 + mine * bz, bz), target], local_sem
+        )
+
     def open_up():
-        source, target = spans(mine)
-        own = pltpu.make_async_copy(
-            p_ref.at[:, source], m_ref.at[pl.ds(1 + mine * bz, bz), target], local_sem
-        )
+        for g in range(groups):
+            main(mine, g).start()
         started(has_down, down(mine))
         started(has_up, up(mine))
-        for g in range(groups):
-            main(mine, g).start()
-        own.start()
-        own.wait()
+        own().wait()
         halo_in(mine)
         for g in range(groups):
             pack(mine, g)
@@ -287,7 +288,7 @@
                 left(has_right, rightward(brick, g))
             left(has_left, leftward(brick))
 
-    return open_up, columns_in, close
+    return open_up, columns_in, close, own
 
 
 def render(
@@ -315,31 +316,6 @@
             )
         )
     ]
-    for copy in tables:
-        copy.start()
-
-    empty = jnp.zeros((tall, LANES), jnp.float32)
-    for ref in (m_ref, h_ref):
-        ref[0] = empty
-        ref[depth + 1] = empty
-
-    @pl.when(jnp.logical_and(z == 0, y == 0))
-    def _():
-        m_ref[:, :HALO] = jnp.zeros((depth + 2, HALO, LANES), jnp.float32)
-
-    @pl.when(jnp.logical_and(z == 1, y == ny - 1))
-    def _():
-        m_ref[:, HALO + strip :] = jnp.zeros((depth + 2, SUB, LANES), jnp.float32)
-
-    @pl.when(x == 0)
-    def _():
-        full_in[...] = jnp.zeros(full_in.shape, jnp.float32)
-        rest_in[...] = jnp.zeros(rest_in.shape, jnp.float32)
-
-    @pl.when(x == nx - 1)
-    def _():
-        ends_in[...] = jnp.zeros(ends_in.shape, jnp.float32)
-
     cross = y + 2 * z - 1
     partners = (
         (y >= 0, (1 - z, y, x)),
@@ -358,8 +334,6 @@
             pl.semaphore_signal(barrier, inc=1, device_id=who, device_id_type=MESH)
 
         count = count + there.astype(jnp.int32)
-    pl.semaphore_wait(barrier, count)
-
     steps = [
         exchange(
             dims, mine, (z, y, x), p_ref, m_ref, full_in, rest_in, ends_in, full_out, rest_out,
@@ -367,6 +341,39 @@
         )
         for mine in range(2)
     ]
+
+    for mine in range(2):
+
+        @pl.when(z == mine)
+        def _():
+            steps[mine][3]().start()
+
+    for copy in tables:
+        copy.start()
+
+    empty = jnp.zeros((tall, LANES), jnp.float32)
+    for ref in (m_ref, h_ref):
+        ref[0] = empty
+        ref[depth + 1] = empty
+
+    @pl.when(jnp.logical_and(z == 0, y == 0))
+    def _():
+        m_ref[:, :HALO] = jnp.zeros((depth + 2, HALO, LANES), jnp.float32)
+
+    @pl.when(jnp.logical_and(z == 1, y == ny - 1))
+    def _():
+        m_ref[:, HALO + strip :] = jnp.zeros((depth + 2, SUB, LANES), jnp.float32)
+
+    @pl.when(x == 0)
+    def _():
+        full_in[...] = jnp.zeros(full_in.shape, jnp.float32)
+        rest_in[...] = jnp.zeros(rest_in.shape, jnp.float32)
+
+    @pl.when(x == nx - 1)
+    def _():
+        ends_in[...] = jnp.zeros(ends_in.shape, jnp.float32)
+
+    pl.semaphore_wait(barrier, count)
 
     for mine in range(2):
 

time: 18.1 us -> 16.9 us (0.934)
  Pallas kernels: 17.1 us -> 15.9 us
    pallas_call x1, Pallas kernels: 17.1 us -> 15.9 us  [two_bricks(): pl.pallas_call(functools.partial(render, dims), out_shape=jax.ShapeDtypeS...]
where the time goes in v4:
time: 16.9 us; the launch traced here: 16.7 us
  Pallas kernels  15.9 us (94%)
  local copies, waits for them, and re-layouts  0.8 us (5%)
    pallas_call x1, Pallas kernels, two_bricks(): pl.pallas_call(functools.partial(render, dims), out_shape=jax.ShapeDtypeS...  15.9 us
    unnamed x1, local copies, waits for them, and re-layouts  0.8 us

profile of v4, /device:TPU:0, one launch (start us, length us, event | category | flops | bytes accessed | tf_op | source)
XLA Modules:
  0.0 16.7 jit_solution(4798860076905697595)
XLA Ops:
  0.0 15.9 %render.1 = f32[4,4,64,128]{3,2,1,0:T(8,128)S(1)} custom-call(f32[4,3]{1,0:T(4,128)} %light_in.1, f32[2,3]{1,0:T(2,128)} %bitcast.10, f32[4]{0:T(128)} %rate_in.1, s32[4,2,8]{2,1,0:T(2,128)} %bitcast.8, s32[2,2,4]{2,1,0:T(2,128)} %bitcast.9, s32[2,4]{1,0:T(2,128)} %bitcast.11, f32[4,128,128]{2,1,0:T(8,128)} %p_ref.1), custom_call_target="tpu_custom_call" | custom-call | tf_op jit(solution)/shard_map/render/pallas_call | solution.py:515
  15.9 0.8 %copy.10 = f32[4,4,1,64,128]{4,3,2,1,0:T(8,128)} copy(f32[4,4,1,64,128]{4,3,2,1,0:T(8,128)S(1)} %bitcast.7) | data formatting | bytes 1048576
